TPU v7x, 256 devices: a whole 4x4x8 slice. The times are simulated.
256 devices in a mesh: row: 8 (over y, core), col: 32 (over z, x).
Axes of the slice: x: 4, y: 4, z: 8, core: 2. Of those that a mesh axis runs over, the one named last changes fastest.
Arguments:
- embeds: bfloat16 [3072, 8192], P('row', 'col'), may hold values from -600 to 600
- ln_gain: float32 [8192], replicated, may hold values from 0.1 to 1.9
- ln_bias: float32 [8192], replicated, may hold values from -3 to 3
- w_qkv: bfloat16 [8192, 24576], P('row', 'col'), may hold values from -4 to 4, as said below
- w_out: bfloat16 [8192, 8192], P('row', 'col'), may hold values from -0.0625 to 0.0625
- out_bias: float32 [8192], P('col'), may hold values from -3 to 3
Outputs:
- attended: bfloat16 [3072, 8192], P('row', 'col')
Inputs may be any that keep to these rules, and one draw needn't show every extreme that they name: Columns of w_qkv are ordered by head, then query, key, value, then entry of the head.
All inputs are finite; a program needn't handle non-finite values.
Results may differ from a plain program's by a relative error of at most 0.0065.
Values may be sent and summed in bfloat16 or wider, within the bound.
A program may use at most 64 MiB of HBM per device.

v0:
```python
import jax
import jax.numpy as jnp
from jax import lax
from jax.sharding import PartitionSpec as P

D = 8192
HEADS = 64
SEQ = 128


def normalize(values, mean, var, gain, shift):
    return ((values - mean) * lax.rsqrt(var + 1e-05) * gain + shift).astype(jnp.bfloat16)


def attend(qkv):
    total, columns = qkv.shape
    head_size = D // HEADS
    heads = columns // (3 * head_size)
    packed = qkv.reshape(total // SEQ, SEQ, heads, 3, head_size)
    query = packed[:, :, :, 0]
    keys = packed[:, :, :, 1]
    vals = packed[:, :, :, 2]
    scores = jnp.einsum("nqhd,nkhd->nhqk", query, keys, preferred_element_type=jnp.float32)
    scores = scores / jnp.sqrt(jnp.float32(head_size))
    peak = jnp.max(scores, axis=-1, keepdims=True)
    expo = jnp.exp(scores - peak)
    probs = (expo / jnp.sum(expo, axis=-1, keepdims=True)).astype(jnp.bfloat16)
    context = jnp.einsum("nhqk,nkhd->nqhd", probs, vals, preferred_element_type=jnp.float32)
    return context.astype(jnp.bfloat16).reshape(total, heads * head_size)


def on_device(embeds, ln_gain, ln_bias, w_qkv, w_out, out_bias):
    width = embeds.shape[1]
    offset = lax.axis_index("col") * width
    values = embeds.astype(jnp.float32)
    gain_part = lax.dynamic_slice_in_dim(ln_gain, offset, width)
    bias_part = lax.dynamic_slice_in_dim(ln_bias, offset, width)
    mean = lax.psum(jnp.sum(values, axis=1), "col")[:, None] / D
    spread = lax.psum(jnp.sum((values - mean) ** 2, axis=1), "col")
    payload = normalize(values, mean, spread[:, None] / D, gain_part, bias_part)
    gathered = lax.all_gather(payload, "col", axis=1, tiled=True)
    left = gathered
    qkv = jnp.dot(
        left, lax.all_gather(w_qkv, "row", axis=0, tiled=True), preferred_element_type=jnp.float32
    )
    context = attend(qkv.astype(jnp.bfloat16))
    full_context = lax.all_gather(context, "col", axis=1, tiled=True)
    left = full_context
    result = jnp.dot(
        left, lax.all_gather(w_out, "row", axis=0, tiled=True), preferred_element_type=jnp.float32
    )
    return (result + out_bias).astype(jnp.bfloat16)


def solution(mesh):
    return jax.shard_map(
        on_device,
        mesh=mesh,
        in_specs=(P("row", "col"), P(), P(), P("row", "col"), P("row", "col"), P("col")),
        out_specs=P("row", "col"),
        check_vma=False,
    )
```

profile of v0, /device:TPU:36, one launch (start us, length us, event | category | flops | bytes accessed | tf_op | source)
XLA Modules:
  0.0 465.9 jit_solution(14634312466143647871)
XLA Ops:
  6.5 0.0 all-gather.5.cloned.1.call-start
  6.5 0.8 dynamic_slice.6
  7.3 0.8 dynamic_slice.7
  8.1 1.1 convert_reduce_fusion
  9.1 66.9 %psum.14 = f32[384]{0:T(512)S(1)} all-reduce(f32[384]{0:T(512)S(1)} %convert_reduce_fusion), channel_id=1, replica_groups=mesh['row'=8,'col'=32] {'col'}, use_global_device_ids=true, to_apply=%region_1.0 | all-reduce | flops 384 | bytes 3072 | tf_op jit(solution)/shard_map/psum | solution.py:38
  76.0 1.2 fusion.7
  77.2 69.6 %psum.15 = f32[384]{0:T(512)S(1)} all-reduce(f32[384]{0:T(512)S(1)} %fusion.7), channel_id=1, replica_groups=mesh['row'=8,'col'=32] {'col'}, use_global_device_ids=true, to_apply=%region_3.0 | all-reduce | flops 384 | bytes 3072 | tf_op jit(solution)/shard_map/psum | solution.py:39
  146.8 1.8 fusion.10
  148.6 0.0 all-gather.5.cloned.1.call-update
  148.6 0.0 all-gather.7.cloned.1.call-start
  148.7 0.7 all-gather.7.cloned.1.call-update
  149.4 0.0 all-gather.11.cloned.1.call-start
  149.4 0.7 all-gather.11.cloned.1.call-update
  150.1 0.0 all-gather.9.cloned.1.call-start
  150.2 98.9 %all-gather.5.cloned.1.call-done = bf16[384,8192]{1,0:T(8,128)(2,1)} async-done(((bf16[384,256]{1,0:T(8,128)(2,1)}), bf16[384,8192]{1,0:T(8,128)(2,1)}) %all-gather.5.cloned.1.call-update) | async-done | bytes 6291472 | tf_op jit(solution)/shard_map/all_gather | solution.py:41
  249.1 70.9 %all-gather.7.cloned.1.call-done = bf16[8192,768]{1,0:T(8,128)(2,1)} async-done(((bf16[1024,768]{1,0:T(8,128)(2,1)}), bf16[8192,768]{1,0:T(8,128)(2,1)}) %all-gather.7.cloned.1.call-update) | async-done | bytes 12582928 | tf_op jit(solution)/shard_map/all_gather | solution.py:44
  320.0 10.8 %convolution_convert_fusion = bf16[384,768]{1,0:T(8,128)(2,1)S(1)} fusion(bf16[384,8192]{1,0:T(8,128)(2,1)} %all-gather.5.cloned.1.call-done, bf16[8192,768]{1,0:T(8,128)(2,1)} %all-gather.7.cloned.1.call-done), kind=kOutput, calls=%fused_computation.1 | convolution fusion | flops 4832133120 | bytes 19464192 | tf_op jit(solution)/shard_map/dot_general | solution.py:43
  330.8 0.0 copy-start
  330.8 0.3 reshape.17
  331.1 0.9 fusion.15
  332.0 0.6 copy.17
  332.6 0.3 fusion.16
  332.9 0.3 convolution_multiply_fusion
  333.1 0.3 fusion.4
  333.4 0.2 copy.15
  333.6 0.7 copy.34
  334.3 0.0 all-gather.9.cloned.1.call-update
  334.3 22.6 %all-gather.11.cloned.1.call-done = bf16[8192,256]{1,0:T(8,128)(2,1)} async-done(((bf16[1024,256]{1,0:T(8,128)(2,1)}), bf16[8192,256]{1,0:T(8,128)(2,1)}) %all-gather.11.cloned.1.call-update) | async-done | bytes 4194320 | tf_op jit(solution)/shard_map/all_gather | solution.py:50
  356.9 96.0 %all-gather.9.cloned.1.call-done = bf16[384,8192]{1,0:T(8,128)(2,1)} async-done(((bf16[384,256]{1,0:T(8,128)(2,1)}), bf16[384,8192]{1,0:T(8,128)(2,1)}) %all-gather.9.cloned.1.call-update) | async-done | bytes 6291472 | tf_op jit(solution)/shard_map/all_gather | solution.py:47
  452.9 0.0 copy-done
  452.9 6.5 %fusion.3 = bf16[384,256]{1,0:T(8,128)(2,1)} fusion(bf16[384,8192]{1,0:T(8,128)(2,1)} %all-gather.9.cloned.1.call-done, bf16[8192,256]{1,0:T(8,128)(2,1)} %all-gather.11.cloned.1.call-done, f32[256]{0:T(256)S(1)} %copy-done), kind=kOutput, calls=%fused_computation.6 | convolution fusion | flops 1610809344 | bytes 10683392 | tf_op jit(solution)/shard_map/dot_general | solution.py:49
  (2 shorter events, 0.0 us)
Async XLA Ops:
  6.5 242.5 %all-gather.5.cloned.1.call-start = ((), (), s32[]{:S(2)}) async-start(), calls=%async_computation | async-start | bytes 6488064 | tf_op jit(solution)/shard_map/all_gather | solution.py:41
  148.6 171.4 %all-gather.7.cloned.1.call-start = ((), (), s32[]{:S(2)}) async-start(), calls=%async_computation.1 | async-start | bytes 14155776 | tf_op jit(solution)/shard_map/all_gather | solution.py:44
  149.4 207.5 %all-gather.11.cloned.1.call-start = ((), (), s32[]{:S(2)}) async-start(), calls=%async_computation.3 | async-start | bytes 4718592 | tf_op jit(solution)/shard_map/all_gather | solution.py:50
  150.1 302.8 %all-gather.9.cloned.1.call-start = ((), (), s32[]{:S(2)}) async-start(), calls=%async_computation.2 | async-start | bytes 6488064 | tf_op jit(solution)/shard_map/all_gather | solution.py:47
  330.8 122.1 %copy-start = (f32[256]{0:T(256)S(1)}, f32[256]{0:T(256)}, u32[]{:S(2)}) copy-start(f32[256]{0:T(256)} %param.11) | copy-start | bytes 3076
Sparse Core Ops, SparseCore 0:
  148.7 100.2 all-gather.4
  250.9 69.0 all-gather.6
  321.9 35.0 all-gather.10
  359.2 93.6 all-gather.8
where the time goes:
time: 466 us
  waiting for transfers between devices  290 us (62%)
  blocking collectives  137 us (29%)
  matrix products  18.1 us (4%)
  between operations  13.2 us (3%)
    all_gather x1, waiting for transfers between devices, on_device(): gathered = lax.all_gather(payload, 'col', axis=1, tiled=True)  98.9 us
    all_gather x1, waiting for transfers between devices, on_device(): full_context = lax.all_gather(context, 'col', axis=1, tiled=True)  96 us
    all_gather x1, waiting for transfers between devices, on_device(): lax.all_gather(w_qkv, 'row', axis=0, tiled=True)  70.9 us
    psum x1, blocking collectives, on_device(): spread = lax.psum(jnp.sum((values - mean) ** 2, axis=1), 'col')  69.6 us
    psum x1, blocking collectives, on_device(): mean = lax.psum(jnp.sum(values, axis=1), 'col')[:, None] / D  66.9 us
    all_gather x1, waiting for transfers between devices, on_device(): lax.all_gather(w_out, 'row', axis=0, tiled=True)  22.6 us
    dot_general x1, matrix products, on_device(): jnp.dot(left, lax.all_gather(w_qkv, 'row', axis=0, tiled=True), preferred...  10.8 us
  transfers between devices with their start and end apart: 4, of which 4 were waited for; matrix products, arithmetic and copies ran while one was open for 3% of the time, Pallas kernels for 0%

commit v1 on v0

--- a/solution.py
+++ b/solution.py
@@ -6,6 +6,11 @@
 D = 8192
 HEADS = 64
 SEQ = 128
+
+
+def gather_and_add(block, mesh_axis):
+    parts = lax.all_gather(block, mesh_axis)
+    return jnp.sum(parts, axis=0)
 
 
 def normalize(values, mean, var, gain, shift):
@@ -35,7 +40,7 @@
     values = embeds.astype(jnp.float32)
     gain_part = lax.dynamic_slice_in_dim(ln_gain, offset, width)
     bias_part = lax.dynamic_slice_in_dim(ln_bias, offset, width)
-    mean = lax.psum(jnp.sum(values, axis=1), "col")[:, None] / D
+    mean = gather_and_add(jnp.sum(values, axis=1), "col")[:, None] / D
     spread = lax.psum(jnp.sum((values - mean) ** 2, axis=1), "col")
     payload = normalize(values, mean, spread[:, None] / D, gain_part, bias_part)
     gathered = lax.all_gather(payload, "col", axis=1, tiled=True)

time: 466 us -> 442 us (0.948)
  blocking collectives: 137 us -> 112 us
    psum x1 -> x0, blocking collectives: 66.9 us -> none  [on_device(): mean = lax.psum(jnp.sum(values, axis=1), 'col')[:, None] / D]
    all_gather x0 -> x1, blocking collectives: none -> 47.2 us  [gather_and_add(): parts = lax.all_gather(block, mesh_axis)]
where the time goes in v1:
time: 442 us; the launch traced here: 441 us
  waiting for transfers between devices  289 us (65%)
  blocking collectives  112 us (25%)
  matrix products  18.1 us (4%)
  between operations  13.2 us (3%)
    all_gather x1, waiting for transfers between devices, on_device(): gathered = lax.all_gather(payload, 'col', axis=1, tiled=True)  98.4 us
    all_gather x1, waiting for transfers between devices, on_device(): full_context = lax.all_gather(context, 'col', axis=1, tiled=True)  96 us
    all_gather x1, waiting for transfers between devices, on_device(): lax.all_gather(w_qkv, 'row', axis=0, tiled=True)  70.9 us
    psum x1, blocking collectives, on_device(): spread = lax.psum(jnp.sum((values - mean) ** 2, axis=1), 'col')  65.2 us
    all_gather x1, blocking collectives, gather_and_add(): parts = lax.all_gather(block, mesh_axis)  47.2 us
    all_gather x1, waiting for transfers between devices, on_device(): lax.all_gather(w_out, 'row', axis=0, tiled=True)  22.6 us
    dot_general x1, matrix products, on_device(): jnp.dot(left, lax.all_gather(w_qkv, 'row', axis=0, tiled=True), preferred...  10.8 us
  transfers between devices with their start and end apart: 4, of which 4 were waited for; matrix products, arithmetic and copies ran while one was open for 3% of the time, Pallas kernels for 0%

profile of v1, /device:TPU:36, one launch (start us, length us, event | category | flops | bytes accessed | tf_op | source)
XLA Modules:
  0.0 441.3 jit_solution(13702997916825083631)
XLA Ops:
  6.5 0.0 all-gather.7.cloned.1.call-start
  6.5 0.8 dynamic_slice.6
  7.3 0.8 dynamic_slice.7
  8.1 1.1 convert_reduce_fusion
  9.1 47.2 %all-gather.1 = f32[32,1,384]{2,1,0:T(1,128)S(1)} all-gather(f32[1,1,384]{2,1,0:T(1,128)S(1)} %reshape.22), channel_id=2, replica_groups=mesh['row'=8,'col'=32] {'col'}, dimensions={0}, use_global_device_ids=true | all-gather | bytes 50688 | tf_op jit(solution)/shard_map/all_gather | solution.py:12
  56.3 0.1 reduce_sum.37
  56.4 1.2 fusion.7
  57.5 65.2 %psum.7 = f32[384]{0:T(512)S(1)} all-reduce(f32[384]{0:T(512)S(1)} %fusion.7), channel_id=1, replica_groups=mesh['row'=8,'col'=32] {'col'}, use_global_device_ids=true, to_apply=%region_3.0 | all-reduce | flops 384 | bytes 3072 | tf_op jit(solution)/shard_map/psum | solution.py:44
  122.7 1.8 fusion.10
  124.5 0.0 all-gather.7.cloned.1.call-update
  124.5 0.0 all-gather.9.cloned.1.call-start
  124.6 0.7 all-gather.9.cloned.1.call-update
  125.3 0.0 all-gather.13.cloned.1.call-start
  125.3 0.7 all-gather.13.cloned.1.call-update
  126.0 0.0 all-gather.11.cloned.1.call-start
  126.1 98.4 %all-gather.7.cloned.1.call-done = bf16[384,8192]{1,0:T(8,128)(2,1)} async-done(((bf16[384,256]{1,0:T(8,128)(2,1)}), bf16[384,8192]{1,0:T(8,128)(2,1)}) %all-gather.7.cloned.1.call-update) | async-done | bytes 6291472 | tf_op jit(solution)/shard_map/all_gather | solution.py:46
  224.4 70.9 %all-gather.9.cloned.1.call-done = bf16[8192,768]{1,0:T(8,128)(2,1)} async-done(((bf16[1024,768]{1,0:T(8,128)(2,1)}), bf16[8192,768]{1,0:T(8,128)(2,1)}) %all-gather.9.cloned.1.call-update) | async-done | bytes 12582928 | tf_op jit(solution)/shard_map/all_gather | solution.py:49
  295.4 10.8 %convolution_convert_fusion = bf16[384,768]{1,0:T(8,128)(2,1)S(1)} fusion(bf16[384,8192]{1,0:T(8,128)(2,1)} %all-gather.7.cloned.1.call-done, bf16[8192,768]{1,0:T(8,128)(2,1)} %all-gather.9.cloned.1.call-done), kind=kOutput, calls=%fused_computation.1 | convolution fusion | flops 4832133120 | bytes 19464192 | tf_op jit(solution)/shard_map/dot_general | solution.py:48
  306.1 0.0 copy-start
  306.2 0.3 reshape.19
  306.5 0.9 fusion.15
  307.3 0.6 copy.22
  307.9 0.3 fusion.16
  308.2 0.3 convolution_multiply_fusion
  308.5 0.3 fusion.4
  308.8 0.2 copy.20
  308.9 0.7 copy.39
  309.7 0.0 all-gather.11.cloned.1.call-update
  309.7 22.6 %all-gather.13.cloned.1.call-done = bf16[8192,256]{1,0:T(8,128)(2,1)} async-done(((bf16[1024,256]{1,0:T(8,128)(2,1)}), bf16[8192,256]{1,0:T(8,128)(2,1)}) %all-gather.13.cloned.1.call-update) | async-done | bytes 4194320 | tf_op jit(solution)/shard_map/all_gather | solution.py:55
  332.3 96.0 %all-gather.11.cloned.1.call-done = bf16[384,8192]{1,0:T(8,128)(2,1)} async-done(((bf16[384,256]{1,0:T(8,128)(2,1)}), bf16[384,8192]{1,0:T(8,128)(2,1)}) %all-gather.11.cloned.1.call-update) | async-done | bytes 6291472 | tf_op jit(solution)/shard_map/all_gather | solution.py:52
  428.3 0.0 copy-done
  428.3 6.5 %fusion.3 = bf16[384,256]{1,0:T(8,128)(2,1)} fusion(bf16[384,8192]{1,0:T(8,128)(2,1)} %all-gather.11.cloned.1.call-done, bf16[8192,256]{1,0:T(8,128)(2,1)} %all-gather.13.cloned.1.call-done, f32[256]{0:T(256)S(1)} %copy-done), kind=kOutput, calls=%fused_computation.6 | convolution fusion | flops 1610809344 | bytes 10683392 | tf_op jit(solution)/shard_map/dot_general | solution.py:54
  (3 shorter events, 0.0 us)
Async XLA Ops:
  6.5 217.9 %all-gather.7.cloned.1.call-start = ((), (), s32[]{:S(2)}) async-start(), calls=%async_computation | async-start | bytes 6488064 | tf_op jit(solution)/shard_map/all_gather | solution.py:46
  124.5 170.8 %all-gather.9.cloned.1.call-start = ((), (), s32[]{:S(2)}) async-start(), calls=%async_computation.1 | async-start | bytes 14155776 | tf_op jit(solution)/shard_map/all_gather | solution.py:49
  125.3 207.0 %all-gather.13.cloned.1.call-start = ((), (), s32[]{:S(2)}) async-start(), calls=%async_computation.3 | async-start | bytes 4718592 | tf_op jit(solution)/shard_map/all_gather | solution.py:55
  126.0 302.3 %all-gather.11.cloned.1.call-start = ((), (), s32[]{:S(2)}) async-start(), calls=%async_computation.2 | async-start | bytes 6488064 | tf_op jit(solution)/shard_map/all_gather | solution.py:52
  306.1 122.2 %copy-start = (f32[256]{0:T(256)S(1)}, f32[256]{0:T(256)}, u32[]{:S(2)}) copy-start(f32[256]{0:T(256)} %param.11) | copy-start | bytes 3076
Sparse Core Ops, SparseCore 0:
  124.7 99.7 all-gather.6
  226.3 69.0 all-gather.8
  297.2 35.0 all-gather.12
  334.6 93.6 all-gather.10

commit v2 on v0

--- a/solution.py
+++ b/solution.py
@@ -38,7 +38,10 @@
     mean = lax.psum(jnp.sum(values, axis=1), "col")[:, None] / D
     spread = lax.psum(jnp.sum((values - mean) ** 2, axis=1), "col")
     payload = normalize(values, mean, spread[:, None] / D, gain_part, bias_part)
-    gathered = lax.all_gather(payload, "col", axis=1, tiled=True)
+    count = lax.axis_size("col")
+    blocks = jnp.stack([payload for _ in range(count)])
+    blocks = lax.all_to_all(blocks, "col", split_axis=0, concat_axis=0)
+    gathered = jnp.concatenate(blocks, axis=1)
     left = gathered
     qkv = jnp.dot(
         left, lax.all_gather(w_qkv, "row", axis=0, tiled=True), preferred_element_type=jnp.float32

time: 466 us -> 403 us (0.86)
  waiting for transfers between devices: 290 us -> 196 us
  starting transfers between devices: 0.12 us -> 23.4 us
    all_gather x1 -> x0, waiting for transfers between devices: 98.9 us -> none  [on_device(): gathered = lax.all_gather(payload, 'col', axis=1, tiled=True)]
    all_to_all x0 -> x1, waiting for transfers between devices: none -> 98 us  [on_device(): blocks = lax.all_to_all(blocks, 'col', split_axis=0, concat_axis=0)]
    all_gather x1, waiting for transfers between devices: 70.9 us -> 0.01 us  [on_device(): lax.all_gather(w_qkv, 'row', axis=0, tiled=True)]
    all_to_all x0 -> x1, starting transfers between devices: none -> 23.3 us  [on_device(): blocks = lax.all_to_all(blocks, 'col', split_axis=0, concat_axis=0)]
    all_gather x1, waiting for transfers between devices: 22.6 us -> 0.02 us  [on_device(): lax.all_gather(w_out, 'row', axis=0, tiled=True)]
  transfers between devices with their start and end apart: 4 -> 4, of which waited for: 4 -> 2; matrix products, arithmetic and copies ran while one was open for 3% -> 6% of each run, Pallas kernels for 0% -> 0%
where the time goes in v2:
time: 403 us
  waiting for transfers between devices  196 us (49%)
  blocking collectives  140 us (35%)
  starting transfers between devices  23.4 us (6%)
  matrix products  18.8 us (5%)
  between operations  13.2 us (3%)
  local copies, waits for them, and re-layouts  7.84 us (2%)
    all_to_all x1, waiting for transfers between devices, on_device(): blocks = lax.all_to_all(blocks, 'col', split_axis=0, concat_axis=0)  98 us
    all_gather x1, waiting for transfers between devices, on_device(): full_context = lax.all_gather(context, 'col', axis=1, tiled=True)  96.9 us
    psum x1, blocking collectives, on_device(): spread = lax.psum(jnp.sum((values - mean) ** 2, axis=1), 'col')  73.2 us
    psum x1, blocking collectives, on_device(): mean = lax.psum(jnp.sum(values, axis=1), 'col')[:, None] / D  66.9 us
    all_to_all x1, starting transfers between devices, on_device(): blocks = lax.all_to_all(blocks, 'col', split_axis=0, concat_axis=0)  23.3 us
    dot_general x1, matrix products, on_device(): jnp.dot(left, lax.all_gather(w_qkv, 'row', axis=0, tiled=True), preferred...  11.5 us
  transfers between devices with their start and end apart: 4, of which 2 were waited for; matrix products, arithmetic and copies ran while one was open for 6% of the time, Pallas kernels for 0%

profile of v2, /device:TPU:36, one launch (start us, length us, event | category | flops | bytes accessed | tf_op | source)
XLA Modules:
  0.0 403.1 jit_solution(5428748751274947983)
XLA Ops:
  6.5 0.0 all-gather.4.cloned.1.call-start
  6.5 0.7 all-gather.4.cloned.1.call-update
  7.3 0.8 dynamic_slice.6
  8.0 0.8 dynamic_slice.7
  8.8 1.1 convert_reduce_fusion
  9.9 66.9 %psum.14 = f32[384]{0:T(512)S(1)} all-reduce(f32[384]{0:T(512)S(1)} %convert_reduce_fusion), channel_id=1, replica_groups=mesh['row'=8,'col'=32] {'col'}, use_global_device_ids=true, to_apply=%region_1.0 | all-reduce | flops 384 | bytes 3072 | tf_op jit(solution)/shard_map/psum | solution.py:38
  76.8 1.2 fusion.7
  77.9 73.2 %psum.15 = f32[384]{0:T(512)S(1)} all-reduce(f32[384]{0:T(512)S(1)} %fusion.7), channel_id=1, replica_groups=mesh['row'=8,'col'=32] {'col'}, use_global_device_ids=true, to_apply=%region_3.0 | all-reduce | flops 384 | bytes 3072 | tf_op jit(solution)/shard_map/psum | solution.py:39
  151.1 1.1 fusion.10
  152.3 0.2 copy.11
  152.4 3.5 stack.2
  156.0 23.3 %all-to-all-start = ((bf16[32,384,256]{1,2,0:T(8,128)(2,1)}), bf16[32,384,256]{1,2,0:T(8,128)(2,1)}, u32[]{:S(2)}, u32[]{:S(2)}) async-start(bf16[32,384,256]{1,2,0:T(8,128)(2,1)} %stack.2), calls=%async_computation | async-start | bytes 12582912 | tf_op jit(solution)/shard_map/all_to_all | solution.py:43
  179.3 0.0 all-gather.8.cloned.1.call-start
  179.3 0.7 all-gather.8.cloned.1.call-update
  180.1 0.0 all-gather.6.cloned.1.call-start
  180.1 98.0 %all-to-all-done = bf16[32,384,256]{1,2,0:T(8,128)(2,1)} async-done(((bf16[32,384,256]{1,2,0:T(8,128)(2,1)}), bf16[32,384,256]{1,2,0:T(8,128)(2,1)}, u32[]{:S(2)}, u32[]{:S(2)}) %all-to-all-start) | async-done | bytes 6291488 | tf_op jit(solution)/shard_map/all_to_all | solution.py:43
  278.1 0.0 all-gather.4.cloned.1.call-done
  278.1 11.5 %convolution_convert_fusion = bf16[384,768]{1,0:T(8,128)(2,1)S(1)} fusion(bf16[384,8192]{0,1:T(8,128)(2,1)} %bitcast.1, bf16[8192,768]{1,0:T(8,128)(2,1)} %all-gather.4.cloned.1.call-done), kind=kOutput, calls=%fused_computation.1 | convolution fusion | flops 4832133120 | bytes 19464192 | tf_op jit(solution)/shard_map/dot_general | solution.py:46
  289.6 0.0 copy-start
  289.6 0.3 reshape.27
  289.9 0.9 fusion.15
  290.7 0.6 copy.18
  291.3 0.3 fusion.16
  291.7 0.3 convolution_multiply_fusion
  291.9 0.3 fusion.4
  292.2 0.2 copy.16
  292.4 0.7 copy.35
  293.1 0.0 all-gather.6.cloned.1.call-update
  293.1 0.0 all-gather.8.cloned.1.call-done
  293.1 96.9 %all-gather.6.cloned.1.call-done = bf16[384,8192]{1,0:T(8,128)(2,1)} async-done(((bf16[384,256]{1,0:T(8,128)(2,1)}), bf16[384,8192]{1,0:T(8,128)(2,1)}) %all-gather.6.cloned.1.call-update) | async-done | bytes 6291472 | tf_op jit(solution)/shard_map/all_gather | solution.py:50
  390.1 0.0 copy-done
  390.1 6.5 %fusion.3 = bf16[384,256]{1,0:T(8,128)(2,1)} fusion(bf16[384,8192]{1,0:T(8,128)(2,1)} %all-gather.6.cloned.1.call-done, bf16[8192,256]{1,0:T(8,128)(2,1)} %all-gather.8.cloned.1.call-done, f32[256]{0:T(256)S(1)} %copy-done), kind=kOutput, calls=%fused_computation.6 | convolution fusion | flops 1610809344 | bytes 10683392 | tf_op jit(solution)/shard_map/dot_general | solution.py:52
  (2 shorter events, 0.0 us)
Async XLA Ops:
  6.5 271.6 %all-gather.4.cloned.1.call-start = ((), (), s32[]{:S(2)}) async-start(), calls=%async_computation.1 | async-start | bytes 14155776 | tf_op jit(solution)/shard_map/all_gather | solution.py:47
  156.0 122.1 %all-to-all-start = ((bf16[32,384,256]{1,2,0:T(8,128)(2,1)}), bf16[32,384,256]{1,2,0:T(8,128)(2,1)}, u32[]{:S(2)}, u32[]{:S(2)}) async-start(bf16[32,384,256]{1,2,0:T(8,128)(2,1)} %stack.2), calls=%async_computation | async-start | bytes 12582912 | tf_op jit(solution)/shard_map/all_to_all | solution.py:43
  179.3 113.8 %all-gather.8.cloned.1.call-start = ((), (), s32[]{:S(2)}) async-start(), calls=%async_computation.3 | async-start | bytes 4718592 | tf_op jit(solution)/shard_map/all_gather | solution.py:53
  180.1 210.0 %all-gather.6.cloned.1.call-start = ((), (), s32[]{:S(2)}) async-start(), calls=%async_computation.2 | async-start | bytes 6488064 | tf_op jit(solution)/shard_map/all_gather | solution.py:50
  289.6 100.5 %copy-start = (f32[256]{0:T(256)S(1)}, f32[256]{0:T(256)}, u32[]{:S(2)}) copy-start(f32[256]{0:T(256)} %param.11) | copy-start | bytes 3076
Sparse Core Ops, SparseCore 0:
  9.2 72.3 all-gather.3
  182.0 35.8 all-gather.7
  293.2 96.7 all-gather.5
